TPU v7x, 256 devices: a whole 4x4x8 slice. The times are simulated.
256 devices in a mesh: grp: 8 (over y, core), dev: 32 (over x, z).
Axes of the slice: x: 4, y: 4, z: 8, core: 2. Of those that a mesh axis runs over, the one named last changes fastest.
Arguments:
- particle_pos: float32 [2, 4194304], P(None, ('grp', 'dev')), may hold values from -1 to 1
- particle_mass: float32 [4194304], P(('grp', 'dev')), may hold values from 0.02 to 0.2
- leaf_counts: int32 [65536], P(('grp', 'dev')), may hold values from 1 to 64, 3145728 in all
Outputs:
- lens_field: float32 [4, 4194304], P(None, ('grp', 'dev'))
Inputs may be any that keep to these rules, and one draw needn't show every extreme that they name: `leaf_counts`: every leaf holds 1 to 64 live particles and some leaf exactly 64; the counts sum to 3145728.
All inputs are finite; a program needn't handle non-finite values. No bound on the sum of `leaf_counts` on one device may be relied on, other than what follows from the above.
Results may differ from a plain program's by a relative error of at most 0.0001.
Values sent between devices are 32-bit elements; how exact they have to be, the bound alone decides.
A program may use at most 192 MiB of HBM per device.

v0:
```python
import jax
import jax.numpy as jnp
from jax import lax
from jax.sharding import PartitionSpec as P

NODES = 6
PPL = 64
LSIDE = 16
SOFTEN = 0.01
PRECISE = lax.Precision.HIGHEST


def partner(block, axis, distance):
    count = lax.axis_size(axis)
    route = []
    for low in range(count):
        high = low | 1 << distance
        if high != low and high < count:
            route += [(low, high), (high, low)]
    return lax.ppermute(block, axis, route)


def node_angles():
    return (2.0 * jnp.arange(NODES, dtype=jnp.float32) + 1.0) * (jnp.pi / (2.0 * NODES))


def cheb_points():
    return jnp.cos(node_angles())


def interp_basis(coords):
    angles = node_angles()
    expand = (slice(None),) + (None,) * coords.ndim
    result = jnp.zeros((NODES,) + coords.shape, jnp.float32) + 1.0 / NODES
    lower_poly = jnp.ones_like(coords)
    upper_poly = coords
    for degree in range(1, NODES):
        at_nodes = jnp.cos(degree * angles)
        result = result + 2.0 / NODES * at_nodes[expand] * upper_poly[None]
        lower_poly, upper_poly = (upper_poly, 2.0 * coords * upper_poly - lower_poly)
    return result


def kernel_vals(delta_x, delta_y):
    inv_r2 = 1.0 / (delta_x * delta_x + delta_y * delta_y + SOFTEN)
    inv_sq = inv_r2 * inv_r2
    return (
        delta_x * inv_r2,
        delta_y * inv_r2,
        (delta_y * delta_y - delta_x * delta_x) * inv_sq,
        -2.0 * delta_x * delta_y * inv_sq,
    )


def far_offsets():
    return [
        (off_x, off_y)
        for off_x in range(-3, 4)
        for off_y in range(-3, 4)
        if max(abs(off_x), abs(off_y)) >= 2
    ]


def transfer_table(half_width, off_x, off_y):
    points = cheb_points()
    node_diff = points[:, None] - points[None, :]
    delta_x = half_width * node_diff[:, None, :, None] - 2.0 * half_width * off_x
    delta_y = half_width * node_diff[None, :, None, :] - 2.0 * half_width * off_y
    kernel_set = kernel_vals(delta_x, delta_y)
    stacked = jnp.stack([term_val for term_val in kernel_set])
    return stacked.reshape(4 * NODES * NODES, NODES * NODES)


def pair_mask(size_x, size_y, off_x, off_y):
    cells_x = jnp.arange(size_x, dtype=jnp.int32)
    cells_y = jnp.arange(size_y, dtype=jnp.int32)
    keep_x = jnp.abs((cells_x + off_x) // 2 - cells_x // 2) <= 1
    keep_y = jnp.abs((cells_y + off_y) // 2 - cells_y // 2) <= 1
    return (keep_x[:, None] & keep_y[None, :]).astype(jnp.float32)


def far_field(padded, size_x, size_y, half_width):
    result = jnp.zeros((4 * NODES * NODES, size_x * size_y), jnp.float32)
    for off_x, off_y in far_offsets():
        shifted = (
            padded[:, 3 + off_x : 3 + off_x + size_x, 3 + off_y : 3 + off_y + size_y]
            * pair_mask(size_x, size_y, off_x, off_y)[None]
        )
        result = result + jnp.dot(
            transfer_table(half_width, off_x, off_y),
            shifted.reshape(NODES * NODES, size_x * size_y),
            precision=PRECISE,
            preferred_element_type=jnp.float32,
        )
    return result.reshape(4, NODES * NODES, size_x, size_y)


def child_table():
    points = cheb_points()
    sides = jnp.arange(2, dtype=jnp.float32)
    coords = -0.5 + sides[:, None] + 0.5 * points[None, :]
    per_side = jnp.transpose(interp_basis(coords), (1, 2, 0))
    product_table = per_side[:, None, :, None, :, None] * per_side[None, :, None, :, None, :]
    return product_table.reshape(2, 2, NODES * NODES, NODES * NODES)


def upward(leaf_grid):
    node_table = child_table()
    size_x = leaf_grid.shape[1] // 2
    size_y = leaf_grid.shape[2] // 2
    result = jnp.zeros((NODES * NODES, size_x * size_y), jnp.float32)
    for side_x in (0, 1):
        for side_y in (0, 1):
            child_part = leaf_grid[:, side_x::2, side_y::2].reshape(NODES * NODES, size_x * size_y)
            result = result + jnp.dot(
                node_table[side_x, side_y].T,
                child_part,
                precision=PRECISE,
                preferred_element_type=jnp.float32,
            )
    return result.reshape(NODES * NODES, size_x, size_y)


def downward(parent_local):
    node_table = child_table()
    size_x = parent_local.shape[2]
    size_y = parent_local.shape[3]
    flat_local = jnp.transpose(parent_local, (1, 0, 2, 3)).reshape(
        NODES * NODES, 4 * size_x * size_y
    )
    row_list = []
    for side_x in (0, 1):
        col_list = []
        for side_y in (0, 1):
            child_part = jnp.dot(
                node_table[side_x, side_y],
                flat_local,
                precision=PRECISE,
                preferred_element_type=jnp.float32,
            )
            col_list.append(child_part.reshape(NODES * NODES, 4, size_x, size_y))
        row_list.append(jnp.stack(col_list, axis=-1))
    stacked = jnp.stack(row_list, axis=3).reshape(NODES * NODES, 4, 2 * size_x, 2 * size_y)
    return jnp.transpose(stacked, (1, 0, 2, 3))


def moments(grid_u, grid_v, grid_w):
    basis_u = interp_basis(grid_u) * grid_w[None]
    basis_v = interp_basis(grid_v)
    result = jnp.einsum("axyp,bxyp->abxy", basis_u, basis_v, precision=PRECISE)
    return result.reshape(NODES * NODES, grid_u.shape[0], grid_u.shape[1])


def near_row(target_u, target_v, near_rows):
    size_y = target_u.shape[0]
    blocks = []
    shift_x = []
    shift_y = []
    for off_x in (-1, 0, 1):
        for off_y in (-1, 0, 1):
            blocks.append(near_rows[:, off_x + 1, off_y + 1 : off_y + 1 + size_y, :])
            shift_x.append(jnp.full((PPL,), -off_x, jnp.float32))
            shift_y.append(jnp.full((PPL,), -off_y, jnp.float32))
    sources = jnp.concatenate(blocks, axis=2)
    delta_x = jnp.concatenate(shift_x)[None, None, :] + 0.5 * (
        target_u[:, :, None] - sources[0][:, None, :]
    )
    delta_y = jnp.concatenate(shift_y)[None, None, :] + 0.5 * (
        target_v[:, :, None] - sources[1][:, None, :]
    )
    weight = sources[2][:, None, :]
    return jnp.stack(
        [jnp.sum(weight * term_val, axis=2) for term_val in kernel_vals(delta_x, delta_y)]
    )


def evaluate_row(target_u, target_v, local_row, near_rows):
    basis_u = interp_basis(target_u)
    basis_v = interp_basis(target_v)
    coeffs = local_row.reshape(4, NODES, NODES, target_u.shape[0])
    half_sum = jnp.einsum("cabq,bqp->caqp", coeffs, basis_v, precision=PRECISE)
    far_part = jnp.sum(half_sum * basis_u[None], axis=1)
    return far_part + near_row(target_u, target_v, near_rows)


def leaves_to_grid(values, axis_pos, bit_count):
    x_bits = (bit_count + 1) // 2
    y_bits = bit_count // 2
    old_shape = values.shape
    split_vals = values.reshape(old_shape[:axis_pos] + (2,) * bit_count + old_shape[axis_pos + 1 :])
    x_dims = [axis_pos + bit_count - 1 - 2 * bit_level for bit_level in range(x_bits - 1, -1, -1)]
    y_dims = [axis_pos + bit_count - 2 - 2 * bit_level for bit_level in range(y_bits - 1, -1, -1)]
    lead_dims = list(range(axis_pos))
    tail_dims = list(range(axis_pos + bit_count, split_vals.ndim))
    permuted = jnp.transpose(split_vals, lead_dims + x_dims + y_dims + tail_dims)
    return permuted.reshape(
        old_shape[:axis_pos] + (2**x_bits, 2**y_bits) + old_shape[axis_pos + 1 :]
    )


def grid_to_leaves(values, axis_pos, bit_count):
    x_bits = (bit_count + 1) // 2
    y_bits = bit_count // 2
    old_shape = values.shape
    split_vals = values.reshape(old_shape[:axis_pos] + (2,) * bit_count + old_shape[axis_pos + 2 :])
    order_dims = []
    for bit_level in range(bit_count - 1, -1, -1):
        if bit_level % 2 == 0:
            order_dims.append(axis_pos + x_bits - 1 - bit_level // 2)
        else:
            order_dims.append(axis_pos + x_bits + y_bits - 1 - (bit_level - 1) // 2)
    lead_dims = list(range(axis_pos))
    tail_dims = list(range(axis_pos + bit_count, split_vals.ndim))
    permuted = jnp.transpose(split_vals, lead_dims + order_dims + tail_dims)
    return permuted.reshape(old_shape[:axis_pos] + (2**bit_count,) + old_shape[axis_pos + 2 :])


def morton_split(code_val, bit_count):
    coord_x = code_val * 0
    coord_y = code_val * 0
    for bit_level in range((bit_count + 1) // 2):
        coord_x = coord_x + code_val // 4**bit_level % 2 * 2**bit_level
        coord_y = coord_y + code_val // (2 * 4**bit_level) % 2 * 2**bit_level
    return (coord_x, coord_y)


def cut_moments(moment_grid, strip_kind):
    if strip_kind == 0:
        return moment_grid[:, :3, :]
    if strip_kind == 1:
        return moment_grid[:, -3:, :]
    if strip_kind == 2:
        return jnp.swapaxes(moment_grid[:, :, :3], 1, 2)
    return jnp.swapaxes(moment_grid[:, :, -3:], 1, 2)


def cut_particles(particles, strip_kind):
    if strip_kind == 0:
        return particles[:, 0]
    if strip_kind == 1:
        return particles[:, -1]
    if strip_kind == 2:
        return particles[:, :, 0]
    return particles[:, :, -1]


def corner(strip_vals, off_x, off_y, use_x):
    along_y = strip_vals[:, :, -3:] if off_y < 0 else strip_vals[:, :, :3]
    along_x = strip_vals[:, :, -3:] if off_x < 0 else strip_vals[:, :, :3]
    return jnp.where(use_x, along_y, jnp.swapaxes(along_x, 1, 2))


def dot_corner(strip_vals, off_x, off_y, use_x):
    from_x = strip_vals[:, -1] if off_y < 0 else strip_vals[:, 0]
    from_y = strip_vals[:, -1] if off_x < 0 else strip_vals[:, 0]
    return jnp.where(use_x, from_x, from_y)[:, None, None]


def swap_bit(values, code_bit, dev_bits):
    if code_bit < dev_bits:
        return partner(values, "dev", code_bit)
    return partner(values, "grp", code_bit - dev_bits)


def on_device(particle_pos, particle_mass, leaf_counts):
    grp_count = lax.axis_size("grp")
    dev_count = lax.axis_size("dev")
    block_bits = (grp_count * dev_count).bit_length() - 1
    dev_bits = dev_count.bit_length() - 1
    local_bits = 2 * (LSIDE.bit_length() - 1)
    side_par = LSIDE // 2
    blocks_x = 2 ** ((block_bits + 1) // 2)
    blocks_y = 2 ** (block_bits // 2)
    live_mask = (jnp.arange(PPL, dtype=jnp.int32)[None, :] < leaf_counts[:, None]).astype(
        jnp.float32
    )
    mass_rows = particle_mass.reshape(LSIDE * LSIDE, PPL)
    mass_sum, live_sum = lax.psum(
        (jnp.sum(mass_rows * live_mask), jnp.sum(live_mask)), ("grp", "dev")
    )
    mean_mass = mass_sum / live_sum
    weights = (mass_rows - mean_mass) * live_mask
    positions = particle_pos.reshape(2, LSIDE * LSIDE, PPL)
    grid_u = leaves_to_grid(positions[0], 0, local_bits)
    grid_v = leaves_to_grid(positions[1], 0, local_bits)
    grid_w = leaves_to_grid(weights, 0, local_bits)
    leaf_moments = moments(grid_u, grid_v, grid_w)
    parent_moments = upward(leaf_moments)
    particles = jnp.stack([grid_u, grid_v, grid_w])
    packed = jnp.stack(
        [
            jnp.concatenate(
                [
                    cut_moments(leaf_moments, strip_kind).ravel(),
                    cut_moments(parent_moments, strip_kind).ravel(),
                    cut_particles(particles, strip_kind).ravel(),
                ]
            )
            for strip_kind in range(4)
        ]
    )
    leaf_len = NODES * NODES * 3 * LSIDE
    par_len = NODES * NODES * 3 * side_par

    def unpack(vector):
        return (
            vector[:leaf_len].reshape(NODES * NODES, 3, LSIDE),
            vector[leaf_len : leaf_len + par_len].reshape(NODES * NODES, 3, side_par),
            vector[leaf_len + par_len :].reshape(3, LSIDE, PPL),
        )

    block_id = lax.axis_index("grp") * dev_count + lax.axis_index("dev")
    block_x, block_y = morton_split(block_id, block_bits)
    x_carry = jnp.stack([packed[1], packed[0]])
    for bit_level in range((block_bits + 1) // 2):
        taken = swap_bit(x_carry, 2 * bit_level, dev_bits)
        low_part = block_x % 2**bit_level
        x_carry = jnp.stack(
            [
                jnp.where(low_part == 0, taken[0], x_carry[0]),
                jnp.where(low_part == 2**bit_level - 1, taken[1], x_carry[1]),
            ]
        )
    y_carry = jnp.stack(
        [
            jnp.stack([packed[3], x_carry[0], x_carry[1]]),
            jnp.stack([packed[2], x_carry[0], x_carry[1]]),
        ]
    )
    for bit_level in range(block_bits // 2):
        taken = swap_bit(y_carry, 2 * bit_level + 1, dev_bits)
        low_part = block_y % 2**bit_level
        y_carry = jnp.stack(
            [
                jnp.where(low_part == 0, taken[0], y_carry[0]),
                jnp.where(low_part == 2**bit_level - 1, taken[1], y_carry[1]),
            ]
        )
    near_vecs = {
        (-1, 0): x_carry[0],
        (1, 0): x_carry[1],
        (0, -1): y_carry[0, 0],
        (0, 1): y_carry[1, 0],
        (-1, -1): y_carry[0, 1],
        (1, -1): y_carry[0, 2],
        (-1, 1): y_carry[1, 1],
        (1, 1): y_carry[1, 2],
    }

    def edge_vector(off_x, off_y):
        return near_vecs[off_x, off_y]

    tile_map = {(0, 0): (leaf_moments, parent_moments, particles)}
    for off_x in (-1, 0, 1):
        for off_y in (-1, 0, 1):
            if off_x == 0 and off_y == 0:
                continue
            near_x = block_x + off_x
            near_y = block_y + off_y
            inside = (
                (near_x >= 0) & (near_x < blocks_x) & (near_y >= 0) & (near_y < blocks_y)
            ).astype(jnp.float32)
            if off_y == 0:
                leaf_part, par_part, dot_part = unpack(edge_vector(off_x, off_y))
                pieces = (leaf_part, par_part, dot_part[:, None])
            elif off_x == 0:
                leaf_part, par_part, dot_part = unpack(edge_vector(off_x, off_y))
                pieces = (
                    jnp.swapaxes(leaf_part, 1, 2),
                    jnp.swapaxes(par_part, 1, 2),
                    dot_part[:, :, None],
                )
            else:
                vector = near_vecs[off_x, off_y]
                use_x = True
                leaf_part, par_part, dot_part = unpack(vector)
                pieces = (
                    corner(leaf_part, off_x, off_y, use_x),
                    corner(par_part, off_x, off_y, use_x),
                    dot_corner(dot_part, off_x, off_y, use_x),
                )
            tile_map[off_x, off_y] = tuple((piece_val * inside for piece_val in pieces))
    windows = []
    for member in range(3):
        columns = [
            jnp.concatenate([tile_map[off_x, off_y][member] for off_y in (-1, 0, 1)], axis=2)
            for off_x in (-1, 0, 1)
        ]
        windows.append(jnp.concatenate(columns, axis=1))
    leaf_window, par_window, part_window = windows
    parent_local = far_field(par_window, side_par, side_par, 1.0)
    leaf_local = far_field(leaf_window, LSIDE, LSIDE, 0.5) + downward(parent_local)

    def one_row(row_idx):
        near_rows = lax.dynamic_slice_in_dim(part_window, row_idx, 3, 1)
        target_u = lax.dynamic_index_in_dim(grid_u, row_idx, 0, keepdims=False)
        target_v = lax.dynamic_index_in_dim(grid_v, row_idx, 0, keepdims=False)
        local_row = lax.dynamic_index_in_dim(leaf_local, row_idx, 2, keepdims=False)
        return evaluate_row(target_u, target_v, local_row, near_rows)

    fields = lax.map(one_row, jnp.arange(LSIDE, dtype=jnp.int32))
    fields = jnp.transpose(fields, (1, 0, 2, 3))
    return grid_to_leaves(fields, 1, local_bits).reshape(4, LSIDE * LSIDE * PPL)


def solution(mesh):
    in_specs = (P(None, ("grp", "dev")), P(("grp", "dev")), P(("grp", "dev")))
    out_specs = P(None, ("grp", "dev"))
    return jax.shard_map(
        on_device, mesh=mesh, in_specs=in_specs, out_specs=out_specs, check_vma=False
    )
```

profile of v0, /device:TPU:1, one launch (start us, length us, event | category | flops | bytes accessed | tf_op | source)
XLA Modules:
  0.0 526.9 jit_solution(16787211099503064006)
XLA Ops:
  5.6 81.5 %all-reduce = (f32[]{:T(128)}, f32[]{:T(128)}) all-reduce(f32[]{:T(128)} %select_reduce_fusion, f32[]{:T(128)} %convert_reduce_fusion), channel_id=1, replica_groups=mesh['grp'=8,'dev'=32] {'grp','dev'}, use_global_device_ids=true, to_apply=%region_1.0 | all-reduce | flops 2 | bytes 16 | tf_op jit(solution)/shard_map/psum | solution.py:278
  88.8 2.6 convolution_bitcast_fusion.1
  98.2 12.1 %collective-permute-start = (f32[2,5664]{1,0:T(2,128)}, f32[2,5664]{1,0:T(2,128)}, u32[]{:S(2)}, u32[]{:S(2)}) collective-permute-start(f32[2,5664]{1,0:T(2,128)} %pad_maximum_fusion.90), channel_id=1, source_target_pairs={{0,1},{1,0},{2,3},{3,2},{4,5},{5,4},{6,7},{7,6},{8,9},{9,8},{10,11... | collective-permute-start | bytes 135944 | tf_op jit(solution)/shard_map/ppermute | solution.py:20
  112.8 2.4 broadcast_multiply_fusion.70
  115.2 3.5 broadcast_multiply_fusion.71
  119.5 3.1 broadcast_multiply_fusion.150
  122.7 4.1 broadcast_multiply_fusion.151
  175.8 3.3 collective-permute-start.1
  179.7 3.3 collective-permute-done.1
  186.9 3.0 collective-permute-done.2
  216.3 2.6 pad_maximum_fusion.2
  218.8 3.4 collective-permute-done.4
  223.5 3.1 collective-permute-done.5
  228.1 6.2 %collective-permute-start.6 = (f32[2,3,5664]{2,1,0:T(4,128)}, f32[2,3,5664]{2,1,0:T(4,128)}, u32[]{:S(2)}, u32[]{:S(2)}) collective-permute-start(f32[2,3,5664]{2,1,0:T(4,128)} %pad_maximum_fusion.82), channel_id=1, source_target_pairs={{0,32},{32,0},{64,96},{96,64},{128,160},{160,128},{192,224},{224,1... | collective-permute-start | bytes 407816 | tf_op jit(solution)/shard_map/ppermute | solution.py:20
  248.5 1.9 reshape.8411
  252.4 1.9 reshape.8403
  254.3 1.9 reshape.8391
  258.1 1.9 reshape.8381
  260.1 1.9 reshape.8377
  262.0 1.9 reshape.8373
  273.5 1.9 reshape.8383
  285.0 1.9 reshape.8399
  286.9 1.9 reshape.8401
  288.9 1.9 reshape.8405
  290.8 1.9 reshape.8409
  294.6 1.9 reshape.8419
  296.6 1.9 reshape.8423
  298.5 1.9 reshape.8425
  323.1 2.0 reshape.8284
  335.0 2.1 collective-permute-start.7
  338.2 4.8 collective-permute-done.7
  381.5 143.4 %while.13 = (s32[]{:T(128)}, f32[16,4,16,64]{3,1,2,0:T(4,128)S(1)}, s32[16]{0:T(128)S(1)}, f32[16,16,64]{2,1,0:T(8,128)S(1)}, f32[4,36,16,16]{1,0,3,2:T(4,128)S(...) while((s32[]{:T(128)}, f32[16,4,16,64]{3,1,2,0:T(4,128)S(1)}, ...), condition=%wide.region_10.11_spmd, body=%wide.region_4.10_spmd.sunk | while | flops 17893484 | bytes 1122444 | solution.py:401
  387.1 3.6 multiply_reduce_fusion.5
  396.0 3.6 multiply_reduce_fusion.5
  405.0 3.6 multiply_reduce_fusion.5
  413.9 3.6 multiply_reduce_fusion.5
  422.8 3.6 multiply_reduce_fusion.5
  431.8 3.6 multiply_reduce_fusion.5
  440.7 3.6 multiply_reduce_fusion.5
  449.7 3.6 multiply_reduce_fusion.5
  458.6 3.6 multiply_reduce_fusion.5
  467.6 3.6 multiply_reduce_fusion.5
  476.5 3.6 multiply_reduce_fusion.5
  485.4 3.6 multiply_reduce_fusion.5
  494.4 3.6 multiply_reduce_fusion.5
  503.3 3.6 multiply_reduce_fusion.5
  512.3 3.6 multiply_reduce_fusion.5
  521.2 3.6 multiply_reduce_fusion.5
  (1131 shorter events, 240.3 us)
Async XLA Ops:
  88.8 8.1 %copy-start.40 = (f32[2,2,2,2,2,2,2,2,64]{8,7,6,5,4,3,2,1,0:T(2,128)}, f32[2,2,2,2,2,2,2,2,64]{8,7,6,5,4,3,2,1,0:T(2,128)S(1)}, u32[]{:S(2)}) copy-start(f32[2,2,2,2,2,2,2,2,64]{8,7,6,5,4,3,2,1,0:T(2,128)S(1)} %copy.346) | copy-start | bytes 196612
  95.5 16.4 %copy-start.47 = (f32[2,2,36,36]{3,2,1,0:T(8,128)}, f32[2,2,36,36]{3,2,1,0:T(8,128)S(1)}, u32[]{:S(2)}) copy-start(f32[2,2,36,36]{3,2,1,0:T(8,128)S(1)} %broadcast_multiply_fusion.153) | copy-start | bytes 62212
  98.2 77.6 %collective-permute-start = (f32[2,5664]{1,0:T(2,128)}, f32[2,5664]{1,0:T(2,128)}, u32[]{:S(2)}, u32[]{:S(2)}) collective-permute-start(f32[2,5664]{1,0:T(2,128)} %pad_maximum_fusion.90), channel_id=1, source_target_pairs={{0,1},{1,0},{2,3},{3,2},{4,5},{5,4},{6,7},{7,6},{8,9},{9,8},{10,11... | collective-permute-start | bytes 135944 | tf_op jit(solution)/shard_map/ppermute | solution.py:20
  175.8 7.1 %collective-permute-start.1 = (f32[2,5664]{1,0:T(2,128)}, f32[2,5664]{1,0:T(2,128)}, u32[]{:S(2)}, u32[]{:S(2)}) collective-permute-start(f32[2,5664]{1,0:T(2,128)} %collective-permute-done), channel_id=1, source_target_pairs={{0,4},{4,0},{1,5},{5,1},{2,6},{6,2},{3,7},{7,3},{8,12},{12,8},{9,1... | collective-permute-start | bytes 135944 | tf_op jit(solution)/shard_map/ppermute | solution.py:20
  185.2 4.7 collective-permute-start.2
  192.1 21.0 %collective-permute-start.3 = (f32[2,5664]{1,0:T(2,128)}, f32[2,5664]{1,0:T(2,128)}, u32[]{:S(2)}, u32[]{:S(2)}) collective-permute-start(f32[2,5664]{1,0:T(2,128)} %pad_maximum_fusion.92), channel_id=1, source_target_pairs={{0,64},{64,0},{32,96},{96,32},{128,192},{192,128},{160,224},{224,1... | collective-permute-start | bytes 135944 | tf_op jit(solution)/shard_map/ppermute | solution.py:20
  214.9 7.3 %collective-permute-start.4 = (f32[2,3,5664]{2,1,0:T(4,128)S(1)}, f32[2,3,5664]{2,1,0:T(4,128)S(1)}, u32[]{:S(2)}, u32[]{:S(2)}) collective-permute-start(f32[2,3,5664]{2,1,0:T(4,128)S(1)} %pad_maximum_fusion.81), channel_id=1, source_target_pairs={{0,2},{2,0},{1,3},{3,1},{4,6},{6,4},{5,7},{7,5},{8,10},{10,8},{9,1... | collective-permute-start | bytes 407816 | tf_op jit(solution)/shard_map/ppermute | solution.py:20
  216.2 6.1 %copy-start.49 = (f32[1,6,6,6,6]{2,1,0,4,3:T(8,128)S(1)}, f32[1,6,6,6,6]{2,1,0,4,3:T(8,128)}, u32[]{:S(2)}) copy-start(f32[1,6,6,6,6]{2,1,0,4,3:T(8,128)} %get-tuple-element.528) | copy-start | bytes 15556
  216.2 6.1 %copy-start.50 = (f32[1,6,6,6,6]{2,1,0,4,3:T(8,128)S(1)}, f32[1,6,6,6,6]{2,1,0,4,3:T(8,128)}, u32[]{:S(2)}) copy-start(f32[1,6,6,6,6]{2,1,0,4,3:T(8,128)} %get-tuple-element.542) | copy-start | bytes 15556
  216.2 6.1 %copy-start.51 = (f32[1,6,6,6,6]{2,1,0,4,3:T(8,128)S(1)}, f32[1,6,6,6,6]{2,1,0,4,3:T(8,128)}, u32[]{:S(2)}) copy-start(f32[1,6,6,6,6]{2,1,0,4,3:T(8,128)} %get-tuple-element.543) | copy-start | bytes 15556
  216.2 6.1 %copy-start.52 = (f32[1,6,6,6,6]{2,1,0,4,3:T(8,128)S(1)}, f32[1,6,6,6,6]{2,1,0,4,3:T(8,128)}, u32[]{:S(2)}) copy-start(f32[1,6,6,6,6]{2,1,0,4,3:T(8,128)} %get-tuple-element.546) | copy-start | bytes 15556
  216.2 6.1 %copy-start.53 = (f32[1,6,6,6,6]{2,1,0,4,3:T(8,128)S(1)}, f32[1,6,6,6,6]{2,1,0,4,3:T(8,128)}, u32[]{:S(2)}) copy-start(f32[1,6,6,6,6]{2,1,0,4,3:T(8,128)} %get-tuple-element.673) | copy-start | bytes 15556
  216.2 6.1 %copy-start.54 = (f32[1,6,6,6,6]{2,1,0,4,3:T(8,128)S(1)}, f32[1,6,6,6,6]{2,1,0,4,3:T(8,128)}, u32[]{:S(2)}) copy-start(f32[1,6,6,6,6]{2,1,0,4,3:T(8,128)} %get-tuple-element.827) | copy-start | bytes 15556
  216.2 6.1 %copy-start.55 = (f32[1,6,6,6,6]{2,1,0,4,3:T(8,128)S(1)}, f32[1,6,6,6,6]{2,1,0,4,3:T(8,128)}, u32[]{:S(2)}) copy-start(f32[1,6,6,6,6]{2,1,0,4,3:T(8,128)} %get-tuple-element.828) | copy-start | bytes 15556
  216.2 6.1 %copy-start.56 = (f32[1,6,6,6,6]{2,1,0,4,3:T(8,128)S(1)}, f32[1,6,6,6,6]{2,1,0,4,3:T(8,128)}, u32[]{:S(2)}) copy-start(f32[1,6,6,6,6]{2,1,0,4,3:T(8,128)} %get-tuple-element.836) | copy-start | bytes 15556
  222.3 4.4 collective-permute-start.5
  228.1 105.8 %collective-permute-start.6 = (f32[2,3,5664]{2,1,0:T(4,128)}, f32[2,3,5664]{2,1,0:T(4,128)}, u32[]{:S(2)}, u32[]{:S(2)}) collective-permute-start(f32[2,3,5664]{2,1,0:T(4,128)} %pad_maximum_fusion.82), channel_id=1, source_target_pairs={{0,32},{32,0},{64,96},{96,64},{128,160},{160,128},{192,224},{224,1... | collective-permute-start | bytes 407816 | tf_op jit(solution)/shard_map/ppermute | solution.py:20
  321.4 3.7 copy-start.35
  322.3 3.7 copy-start.32
  323.1 3.7 copy-start.30
  335.0 8.0 %collective-permute-start.7 = (f32[2,3,5664]{2,1,0:T(4,128)S(1)}, f32[2,3,5664]{2,1,0:T(4,128)S(1)}, u32[]{:S(2)}, u32[]{:S(2)}) collective-permute-start(f32[2,3,5664]{2,1,0:T(4,128)S(1)} %pad_maximum_fusion.83), channel_id=1, source_target_pairs={{0,128},{128,0},{32,160},{160,32},{64,192},{192,64},{96,224},{224,... | collective-permute-start | bytes 407816 | tf_op jit(solution)/shard_map/ppermute | solution.py:20
  345.1 3.0 copy-start.184
  345.1 3.0 copy-start.256
  345.4 3.0 copy-start.175
  345.4 3.0 copy-start.243
  345.7 3.0 copy-start.163
  345.8 3.0 copy-start.242
  346.0 3.0 copy-start.173
  346.1 3.0 copy-start.241
  346.4 3.0 copy-start.172
  346.4 3.0 copy-start.240
  346.7 3.0 copy-start.171
  346.7 3.0 copy-start.239
  347.0 3.0 copy-start.170
  347.0 3.0 copy-start.238
  347.3 3.0 copy-start.169
  347.3 3.0 copy-start.237
  347.6 3.0 copy-start.156
  347.9 3.0 copy-start.167
  348.2 3.0 copy-start.153
  348.2 3.0 copy-start.255
  350.6 3.0 copy-start.161
  350.6 3.0 copy-start.230
  350.9 3.0 copy-start.183
  351.2 3.0 copy-start.160
  351.2 3.0 copy-start.229
  351.5 3.0 copy-start.149
  351.5 3.0 copy-start.228
  (221 other events, 401.4 us)
where the time goes:
time: 537 us; the launch traced here: 527 us
  local copies, waits for them, and re-layouts  160 us (30%)
  other arithmetic  145 us (27%)
  blocking collectives  81.5 us (15%)
  loops' own time  53.4 us (10%)
  matrix products  37.4 us (7%)
  starting transfers between devices  26.2 us (5%)
  waiting for transfers between devices  17.6 us (3%)
  between operations  5.99 us (1%)
    reshape x80, local copies, waits for them, and re-layouts, transfer_table(): return stacked.reshape(4 * NODES * NODES, NODES * NODES)  97.1 us
    psum x1, blocking collectives, on_device(): lax.psum((jnp.sum(mass_rows * live_mask), jnp.sum(live_mask)), ('grp', 'd...  81.5 us
    reduce_sum x16, other arithmetic, near_row(): jnp.sum(weight * term_val, axis=2)  57.3 us
    another operation x1, loops' own time, on_device(): fields = lax.map(one_row, jnp.arange(LSIDE, dtype=jnp.int32))  53.4 us
    another operation x40, other arithmetic, transfer_table(): stacked = jnp.stack([term_val for term_val in kernel_set])  48.1 us
    ppermute x8, starting transfers between devices, partner(): return lax.ppermute(block, axis, route)  26.2 us
    dot_general x80, matrix products, far_field(): jnp.dot(transfer_table(half_width, off_x, off_y), shifted.reshape(NODES *...  24.8 us
    ppermute x8, waiting for transfers between devices, partner(): return lax.ppermute(block, axis, route)  17.6 us
  transfers between devices with their start and end apart: 8, of which 5 were waited for; matrix products, arithmetic and copies ran while one was open for 36% of the time, Pallas kernels for 0%

commit v1 on v0

--- a/solution.py
+++ b/solution.py
@@ -276,7 +276,7 @@
     )
     mass_rows = particle_mass.reshape(LSIDE * LSIDE, PPL)
     mass_sum, live_sum = lax.psum(
-        (jnp.sum(mass_rows * live_mask), jnp.sum(live_mask)), ("grp", "dev")
+        lax.psum((jnp.sum(mass_rows * live_mask), jnp.sum(live_mask)), "grp"), "dev"
     )
     mean_mass = mass_sum / live_sum
     weights = (mass_rows - mean_mass) * live_mask

time: 537 us -> 549 us (1.022)
  starting transfers between devices: 26.2 us -> 34 us
  waiting for transfers between devices: 17.6 us -> 25 us
    ppermute x8, starting transfers between devices: 26.2 us -> 34 us  [partner(): return lax.ppermute(block, axis, route)]
    ppermute x8, waiting for transfers between devices: 17.6 us -> 25 us  [partner(): return lax.ppermute(block, axis, route)]
    psum x1 -> x2, blocking collectives: 81.5 us -> 78.3 us  [the longest x1 62.6 us: on_device(): lax.psum(lax.psum((jnp.sum(mass_rows * live_mask), jnp.sum(live_mask)), '...]
  transfers between devices with their start and end apart: 8 -> 8, of which waited for: 5 -> 5; matrix products, arithmetic and copies ran while one was open for 36% -> 35% of each run, Pallas kernels for 0% -> 0%
where the time goes in v1:
time: 549 us; the launch traced here: 539 us
  local copies, waits for them, and re-layouts  160 us (29%)
  other arithmetic  145 us (26%)
  blocking collectives  78.3 us (14%)
  loops' own time  53.4 us (10%)
  matrix products  37.4 us (7%)
  starting transfers between devices  34 us (6%)
  waiting for transfers between devices  25 us (5%)
  between operations  6.16 us (1%)
    reshape x80, local copies, waits for them, and re-layouts, transfer_table(): return stacked.reshape(4 * NODES * NODES, NODES * NODES)  97.2 us
    psum x1, blocking collectives, on_device(): lax.psum(lax.psum((jnp.sum(mass_rows * live_mask), jnp.sum(live_mask)), '...  62.6 us
    reduce_sum x16, other arithmetic, near_row(): jnp.sum(weight * term_val, axis=2)  57.3 us
    another operation x1, loops' own time, on_device(): fields = lax.map(one_row, jnp.arange(LSIDE, dtype=jnp.int32))  53.4 us
    another operation x40, other arithmetic, transfer_table(): stacked = jnp.stack([term_val for term_val in kernel_set])  47.9 us
    ppermute x8, starting transfers between devices, partner(): return lax.ppermute(block, axis, route)  34 us
    ppermute x8, waiting for transfers between devices, partner(): return lax.ppermute(block, axis, route)  25 us
    dot_general x80, matrix products, far_field(): jnp.dot(transfer_table(half_width, off_x, off_y), shifted.reshape(NODES *...  24.8 us
  transfers between devices with their start and end apart: 8, of which 5 were waited for; matrix products, arithmetic and copies ran while one was open for 35% of the time, Pallas kernels for 0%

profile of v1, /device:TPU:1, one launch (start us, length us, event | category | flops | bytes accessed | tf_op | source)
XLA Modules:
  0.0 538.9 jit_solution(12764998887180235161)
XLA Ops:
  5.6 15.7 %all-reduce.1 = (f32[]{:T(128)}, f32[]{:T(128)}) all-reduce(f32[]{:T(128)} %select_reduce_fusion, f32[]{:T(128)} %convert_reduce_fusion), channel_id=1, replica_groups=mesh['grp'=8,'dev'=32] {'grp'}, use_global_device_ids=true, to_apply=%region_1.0 | all-reduce | flops 2 | bytes 16 | tf_op jit(solution)/shard_map/psum | solution.py:279
  21.3 62.6 %all-reduce = (f32[]{:T(128)}, f32[]{:T(128)}) all-reduce(f32[]{:T(128)} %get-tuple-element.204, f32[]{:T(128)} %get-tuple-element.205), channel_id=1, replica_groups=mesh['grp'=8,'dev'=32] {'dev'}, use_global_device_ids=true, to_apply=%region_2.0 | all-reduce | flops 2 | bytes 16 | tf_op jit(solution)/shard_map/psum | solution.py:278
  85.8 2.6 convolution_bitcast_fusion.1
  95.2 11.5 %collective-permute-start = (f32[2,5664]{1,0:T(2,128)}, f32[2,5664]{1,0:T(2,128)}, u32[]{:S(2)}, u32[]{:S(2)}) collective-permute-start(f32[2,5664]{1,0:T(2,128)} %pad_maximum_fusion.90), channel_id=1, source_target_pairs={{0,1},{1,0},{2,3},{3,2},{4,5},{5,4},{6,7},{7,6},{8,9},{9,8},{10,11... | collective-permute-start | bytes 135944 | tf_op jit(solution)/shard_map/ppermute | solution.py:20
  109.0 2.4 broadcast_multiply_fusion.70
  111.4 3.5 broadcast_multiply_fusion.71
  115.8 3.1 broadcast_multiply_fusion.150
  118.9 4.1 broadcast_multiply_fusion.151
  172.5 6.5 %collective-permute-done.1 = f32[2,5664]{1,0:T(2,128)} collective-permute-done((f32[2,5664]{1,0:T(2,128)}, f32[2,5664]{1,0:T(2,128)}, u32[]{:S(2)}, u32[]{:S(2)}) %collective-permute-start.1) | collective-permute-done | bytes 45344 | tf_op jit(solution)/shard_map/ppermute | solution.py:20
  181.8 4.1 collective-permute-done.2
  211.2 2.6 pad_maximum_fusion.2
  213.8 4.5 collective-permute-done.4
  219.6 3.1 collective-permute-done.5
  224.1 22.1 %collective-permute-start.6 = (f32[2,3,5664]{2,1,0:T(4,128)}, f32[2,3,5664]{2,1,0:T(4,128)}, u32[]{:S(2)}, u32[]{:S(2)}) collective-permute-start(f32[2,3,5664]{2,1,0:T(4,128)} %pad_maximum_fusion.82), channel_id=1, source_target_pairs={{0,32},{32,0},{64,96},{96,64},{128,160},{160,128},{192,224},{224,1... | collective-permute-start | bytes 407816 | tf_op jit(solution)/shard_map/ppermute | solution.py:20
  247.1 1.9 reshape.8445
  250.9 1.9 reshape.8435
  254.8 1.9 reshape.8427
  256.7 1.9 reshape.8421
  262.4 1.9 reshape.8407
  264.4 1.9 reshape.8403
  270.1 1.9 reshape.8381
  272.0 1.9 reshape.8377
  275.9 1.9 reshape.8365
  281.7 1.9 reshape.8375
  289.3 1.9 reshape.8389
  291.3 1.9 reshape.8393
  293.2 1.9 reshape.8395
  295.1 1.9 reshape.8397
  299.0 1.9 reshape.8401
  335.1 2.0 reshape.8284
  348.4 6.6 %collective-permute-done.7 = f32[2,3,5664]{2,1,0:T(4,128)S(1)} collective-permute-done((f32[2,3,5664]{2,1,0:T(4,128)S(1)}, f32[2,3,5664]{2,1,0:T(4,128)S(1)}, u32[]{:S(2)}, u32[]{:S(2)}) %collective-permute-start.7) | collective-permute-done | bytes 135968 | tf_op jit(solution)/shard_map/ppermute | solution.py:20
  393.5 143.4 %while.13 = (s32[]{:T(128)}, f32[16,4,16,64]{3,1,2,0:T(4,128)S(1)}, s32[16]{0:T(128)S(1)}, f32[16,16,64]{2,1,0:T(8,128)S(1)}, f32[4,36,16,16]{1,0,3,2:T(4,128)S(...) while((s32[]{:T(128)}, f32[16,4,16,64]{3,1,2,0:T(4,128)S(1)}, ...), condition=%wide.region_12.13_spmd, body=%wide.region_6.12_spmd.sunk | while | flops 17893484 | bytes 1122444 | solution.py:401
  399.1 3.6 multiply_reduce_fusion.5
  408.0 3.6 multiply_reduce_fusion.5
  417.0 3.6 multiply_reduce_fusion.5
  425.9 3.6 multiply_reduce_fusion.5
  434.9 3.6 multiply_reduce_fusion.5
  443.8 3.6 multiply_reduce_fusion.5
  452.7 3.6 multiply_reduce_fusion.5
  461.7 3.6 multiply_reduce_fusion.5
  470.6 3.6 multiply_reduce_fusion.5
  479.6 3.6 multiply_reduce_fusion.5
  488.5 3.6 multiply_reduce_fusion.5
  497.5 3.6 multiply_reduce_fusion.5
  506.4 3.6 multiply_reduce_fusion.5
  515.3 3.6 multiply_reduce_fusion.5
  524.3 3.6 multiply_reduce_fusion.5
  533.2 3.6 multiply_reduce_fusion.5
  (1132 shorter events, 236.2 us)
Async XLA Ops:
  85.8 8.1 %copy-start.40 = (f32[2,2,2,2,2,2,2,2,64]{8,7,6,5,4,3,2,1,0:T(2,128)}, f32[2,2,2,2,2,2,2,2,64]{8,7,6,5,4,3,2,1,0:T(2,128)S(1)}, u32[]{:S(2)}) copy-start(f32[2,2,2,2,2,2,2,2,64]{8,7,6,5,4,3,2,1,0:T(2,128)S(1)} %copy.346) | copy-start | bytes 196612
  92.4 15.8 %copy-start.47 = (f32[2,2,36,36]{3,2,1,0:T(8,128)}, f32[2,2,36,36]{3,2,1,0:T(8,128)S(1)}, u32[]{:S(2)}) copy-start(f32[2,2,36,36]{3,2,1,0:T(8,128)S(1)} %broadcast_multiply_fusion.153) | copy-start | bytes 62212
  95.2 76.7 %collective-permute-start = (f32[2,5664]{1,0:T(2,128)}, f32[2,5664]{1,0:T(2,128)}, u32[]{:S(2)}, u32[]{:S(2)}) collective-permute-start(f32[2,5664]{1,0:T(2,128)} %pad_maximum_fusion.90), channel_id=1, source_target_pairs={{0,1},{1,0},{2,3},{3,2},{4,5},{5,4},{6,7},{7,6},{8,9},{9,8},{10,11... | collective-permute-start | bytes 135944 | tf_op jit(solution)/shard_map/ppermute | solution.py:20
  171.9 7.1 %collective-permute-start.1 = (f32[2,5664]{1,0:T(2,128)}, f32[2,5664]{1,0:T(2,128)}, u32[]{:S(2)}, u32[]{:S(2)}) collective-permute-start(f32[2,5664]{1,0:T(2,128)} %collective-permute-done), channel_id=1, source_target_pairs={{0,4},{4,0},{1,5},{5,1},{2,6},{6,2},{3,7},{7,3},{8,12},{12,8},{9,1... | collective-permute-start | bytes 135944 | tf_op jit(solution)/shard_map/ppermute | solution.py:20
  181.2 4.7 collective-permute-start.2
  188.2 20.9 %collective-permute-start.3 = (f32[2,5664]{1,0:T(2,128)}, f32[2,5664]{1,0:T(2,128)}, u32[]{:S(2)}, u32[]{:S(2)}) collective-permute-start(f32[2,5664]{1,0:T(2,128)} %pad_maximum_fusion.92), channel_id=1, source_target_pairs={{0,64},{64,0},{32,96},{96,32},{128,192},{192,128},{160,224},{224,1... | collective-permute-start | bytes 135944 | tf_op jit(solution)/shard_map/ppermute | solution.py:20
  211.0 7.3 %collective-permute-start.4 = (f32[2,3,5664]{2,1,0:T(4,128)S(1)}, f32[2,3,5664]{2,1,0:T(4,128)S(1)}, u32[]{:S(2)}, u32[]{:S(2)}) collective-permute-start(f32[2,3,5664]{2,1,0:T(4,128)S(1)} %pad_maximum_fusion.81), channel_id=1, source_target_pairs={{0,2},{2,0},{1,3},{3,1},{4,6},{6,4},{5,7},{7,5},{8,10},{10,8},{9,1... | collective-permute-start | bytes 407816 | tf_op jit(solution)/shard_map/ppermute | solution.py:20
  211.1 7.2 %copy-start.49 = (f32[1,6,6,6,6]{2,1,0,4,3:T(8,128)S(1)}, f32[1,6,6,6,6]{2,1,0,4,3:T(8,128)}, u32[]{:S(2)}) copy-start(f32[1,6,6,6,6]{2,1,0,4,3:T(8,128)} %get-tuple-element.530) | copy-start | bytes 15556
  211.1 7.2 %copy-start.50 = (f32[1,6,6,6,6]{2,1,0,4,3:T(8,128)S(1)}, f32[1,6,6,6,6]{2,1,0,4,3:T(8,128)}, u32[]{:S(2)}) copy-start(f32[1,6,6,6,6]{2,1,0,4,3:T(8,128)} %get-tuple-element.544) | copy-start | bytes 15556
  211.1 7.2 %copy-start.51 = (f32[1,6,6,6,6]{2,1,0,4,3:T(8,128)S(1)}, f32[1,6,6,6,6]{2,1,0,4,3:T(8,128)}, u32[]{:S(2)}) copy-start(f32[1,6,6,6,6]{2,1,0,4,3:T(8,128)} %get-tuple-element.545) | copy-start | bytes 15556
  211.1 7.2 %copy-start.52 = (f32[1,6,6,6,6]{2,1,0,4,3:T(8,128)S(1)}, f32[1,6,6,6,6]{2,1,0,4,3:T(8,128)}, u32[]{:S(2)}) copy-start(f32[1,6,6,6,6]{2,1,0,4,3:T(8,128)} %get-tuple-element.548) | copy-start | bytes 15556
  211.1 7.2 %copy-start.53 = (f32[1,6,6,6,6]{2,1,0,4,3:T(8,128)S(1)}, f32[1,6,6,6,6]{2,1,0,4,3:T(8,128)}, u32[]{:S(2)}) copy-start(f32[1,6,6,6,6]{2,1,0,4,3:T(8,128)} %get-tuple-element.675) | copy-start | bytes 15556
  211.1 7.2 %copy-start.54 = (f32[1,6,6,6,6]{2,1,0,4,3:T(8,128)S(1)}, f32[1,6,6,6,6]{2,1,0,4,3:T(8,128)}, u32[]{:S(2)}) copy-start(f32[1,6,6,6,6]{2,1,0,4,3:T(8,128)} %get-tuple-element.829) | copy-start | bytes 15556
  211.2 7.2 %copy-start.55 = (f32[1,6,6,6,6]{2,1,0,4,3:T(8,128)S(1)}, f32[1,6,6,6,6]{2,1,0,4,3:T(8,128)}, u32[]{:S(2)}) copy-start(f32[1,6,6,6,6]{2,1,0,4,3:T(8,128)} %get-tuple-element.830) | copy-start | bytes 15556
  211.2 7.2 %copy-start.56 = (f32[1,6,6,6,6]{2,1,0,4,3:T(8,128)S(1)}, f32[1,6,6,6,6]{2,1,0,4,3:T(8,128)}, u32[]{:S(2)}) copy-start(f32[1,6,6,6,6]{2,1,0,4,3:T(8,128)} %get-tuple-element.838) | copy-start | bytes 15556
  218.3 4.4 collective-permute-start.5
  224.1 121.8 %collective-permute-start.6 = (f32[2,3,5664]{2,1,0:T(4,128)}, f32[2,3,5664]{2,1,0:T(4,128)}, u32[]{:S(2)}, u32[]{:S(2)}) collective-permute-start(f32[2,3,5664]{2,1,0:T(4,128)} %pad_maximum_fusion.82), channel_id=1, source_target_pairs={{0,32},{32,0},{64,96},{96,64},{128,160},{160,128},{192,224},{224,1... | collective-permute-start | bytes 407816 | tf_op jit(solution)/shard_map/ppermute | solution.py:20
  333.4 3.7 copy-start.35
  334.3 3.7 copy-start.32
  335.1 3.7 copy-start.30
  347.0 8.0 %collective-permute-start.7 = (f32[2,3,5664]{2,1,0:T(4,128)S(1)}, f32[2,3,5664]{2,1,0:T(4,128)S(1)}, u32[]{:S(2)}, u32[]{:S(2)}) collective-permute-start(f32[2,3,5664]{2,1,0:T(4,128)S(1)} %pad_maximum_fusion.83), channel_id=1, source_target_pairs={{0,128},{128,0},{32,160},{160,32},{64,192},{192,64},{96,224},{224,... | collective-permute-start | bytes 407816 | tf_op jit(solution)/shard_map/ppermute | solution.py:20
  357.1 3.0 copy-start.184
  357.1 3.0 copy-start.256
  357.4 3.0 copy-start.175
  357.5 3.0 copy-start.243
  357.8 3.0 copy-start.163
  357.8 3.0 copy-start.242
  358.1 3.0 copy-start.173
  358.1 3.0 copy-start.241
  358.4 3.0 copy-start.172
  358.4 3.0 copy-start.240
  358.7 3.0 copy-start.171
  358.7 3.0 copy-start.239
  359.0 3.0 copy-start.170
  359.0 3.0 copy-start.238
  359.3 3.0 copy-start.169
  359.3 3.0 copy-start.237
  359.6 3.0 copy-start.156
  359.9 3.0 copy-start.167
  360.2 3.0 copy-start.153
  360.2 3.0 copy-start.255
  360.5 3.0 copy-start.166
  360.8 3.0 copy-start.152
  362.9 3.0 copy-start.183
  363.2 3.0 copy-start.160
  363.2 3.0 copy-start.229
  363.5 3.0 copy-start.149
  363.5 3.0 copy-start.228
  (221 other events, 399.2 us)
